TPU v7x, 256 devices: a whole 4x4x8 slice. The times are simulated.
256 devices in a mesh: row: 32 (over y, x, core), col: 8 (over z).
Axes of the slice: x: 4, y: 4, z: 8, core: 2. Of those that a mesh axis runs over, the one named last changes fastest.
Arguments:
- lead_block: float32 [1024, 1024], P('row'), may hold values from -1 to 3, as said below
- panel_block: float32 [16384, 1024], P('row'), may hold values from -1 to 1
- trailing_slab: float32 [16384, 4096], P('row', 'col'), may hold values from -6 to 6
- charge_lead: float32 [1024, 1024], P('row', 'col'), may hold values from -6 to 6
- charge_rest: float32 [16384, 1024], P('row', 'col'), may hold values from -6 to 6
Outputs:
- lead_factor: float32 [1024, 1024], P('row')
- panel_factor: float32 [16384, 1024], P('row')
- slab_updated: float32 [16384, 4096], P('row', 'col')
- solved_lead: float32 [1024, 1024], P('row', 'col')
- charge_updated: float32 [16384, 1024], P('row', 'col')
Inputs may be any that keep to these rules, and one draw needn't show every extreme that they name: `lead_block`: symmetric positive definite, smallest eigenvalue above 0.4.
All inputs are finite; a program needn't handle non-finite values.
Results may differ from a plain program's by a relative error of at most 0.00014.
Values sent between devices are 32-bit elements; how exact they have to be, the bound alone decides.
A program may use at most 128 MiB of HBM per device.

v0:
```python
import jax
import jax.numpy as jnp
from jax import lax
from jax.sharding import PartitionSpec as P


def broadcast(block, axis, source):
    block = jnp.where(lax.axis_index(axis) == source, block, jnp.zeros_like(block))
    return lax.psum(block, axis)


def factor(matrix):
    half_size = matrix.shape[0] // 2
    first_diag = jnp.linalg.cholesky(matrix[:half_size, :half_size])
    first_below = lax.linalg.triangular_solve(
        first_diag, matrix[half_size:, :half_size], left_side=False, lower=True, transpose_a=True
    )
    schur_block = matrix[half_size:, half_size:] - jnp.dot(
        first_below, first_below.T, precision=lax.Precision.HIGHEST
    )
    second_diag = jnp.linalg.cholesky(schur_block)
    upper_rows = jnp.concatenate([first_diag, jnp.zeros_like(first_diag)], 1)
    lower_rows = jnp.concatenate([first_below, second_diag], 1)
    return jnp.concatenate([upper_rows, lower_rows], 0)


def solve_rows(lead_lower, rows_in):
    return lax.linalg.triangular_solve(
        lead_lower, rows_in, left_side=False, lower=True, transpose_a=True
    )


def shards(lead_block, panel_block, trailing_slab, charge_lead, charge_rest):
    lead_whole, charge_whole = (
        lax.all_gather(lead_block, "row", axis=0, tiled=True),
        lax.all_gather(charge_lead, "row", axis=0, tiled=True),
    )
    lead_lower = factor(lead_whole)
    lower_panel = solve_rows(lead_lower, panel_block)
    far_lower = broadcast(lower_panel, "row", lax.axis_index("col"))
    slab_updated = trailing_slab - jnp.einsum(
        "ik,jk->ij", lower_panel, far_lower, precision=lax.Precision.HIGHEST
    )
    solved_whole = lax.linalg.triangular_solve(lead_lower, charge_whole, left_side=True, lower=True)
    charge_updated = charge_rest - jnp.dot(
        lower_panel, solved_whole, precision=lax.Precision.HIGHEST
    )
    lead_count = lead_block.shape[0]
    lead_offset = lax.axis_index("row") * lead_count
    lead_mine = lax.dynamic_slice_in_dim(lead_lower, lead_offset, lead_count, 0)
    solved_mine = lax.dynamic_slice_in_dim(solved_whole, lead_offset, lead_count, 0)
    return (lead_mine, lower_panel, slab_updated, solved_mine, charge_updated)


def solution(mesh):
    placed = (P("row", None), P("row", None), P("row", "col"), P("row", "col"), P("row", "col"))
    return jax.shard_map(
        shards,
        mesh=mesh,
        in_specs=placed,
        out_specs=(
            P("row", None),
            P("row", None),
            P("row", "col"),
            P("row", "col"),
            P("row", "col"),
        ),
        check_vma=False,
    )
```

profile of v0, /device:TPU:1, one launch (start us, length us, event | category | flops | bytes accessed | tf_op | source)
XLA Modules:
  0.0 583.7 jit_solution(8683999213922054629)
XLA Ops:
  8.0 29.2 %all_gather.7 = f32[1024,128]{1,0:T(8,128)} all-gather(f32[32,128]{1,0:T(8,128)} %param.9), channel_id=1, replica_groups=mesh['row'=32,'col'=8] {'row'}, dimensions={0}, use_global_device_ids=true | all-gather | bytes 540672 | tf_op jit(solution)/shard_map/all_gather | solution.py:36
  37.2 28.6 %all-gather.2.cloned.1.call-done = f32[1024,1024]{1,0:T(8,128)} async-done(((f32[32,1024]{1,0:T(8,128)}), f32[1024,1024]{1,0:T(8,128)}) %all-gather.2.cloned.1.call-update) | async-done | bytes 4194320 | tf_op jit(solution)/shard_map/all_gather | solution.py:35
  65.8 1.3 slice.207
  67.4 1.9 fusion.120
  69.3 11.7 %cholesky.286 = f32[128,128]{1,0:T(8,128)S(1)} custom-call(f32[128,128]{1,0:T(8,128)S(1)} %cholesky.426), custom_call_target="Cholesky" | custom-call | tf_op jit(solution)/shard_map/jit(cholesky)/cholesky | solution.py:14
  81.2 9.8 %custom-call.33 = f32[1,128,128]{1,2,0:T(8,128)S(1)} custom-call(f32[1,128,128]{2,1,0:T(8,128)S(1)} %get-tuple-element.127), custom_call_target="InvertDiagBlocksLowerTriangular" | custom-call | tf_op jit(solution)/shard_map/jit(cholesky)/cholesky | solution.py:14
  91.7 12.1 %cholesky.305 = f32[128,128]{1,0:T(8,128)S(1)} custom-call(f32[128,128]{1,0:T(8,128)S(1)} %cholesky.430), custom_call_target="Cholesky" | custom-call | tf_op jit(solution)/shard_map/jit(cholesky)/cholesky | solution.py:14
  103.9 9.8 %custom-call.34 = f32[1,128,128]{1,2,0:T(8,128)S(1)} custom-call(f32[1,128,128]{2,1,0:T(8,128)S(1)} %get-tuple-element.124), custom_call_target="InvertDiagBlocksLowerTriangular" | custom-call | tf_op jit(solution)/shard_map/jit(cholesky)/cholesky | solution.py:14
  114.4 11.7 %cholesky.326 = f32[128,128]{1,0:T(8,128)S(1)} custom-call(f32[128,128]{1,0:T(8,128)S(1)} %cholesky.435), custom_call_target="Cholesky" | custom-call | tf_op jit(solution)/shard_map/jit(cholesky)/cholesky | solution.py:14
  126.1 9.8 %custom-call.35 = f32[1,128,128]{1,2,0:T(8,128)S(1)} custom-call(f32[1,128,128]{2,1,0:T(8,128)S(1)} %get-tuple-element.121), custom_call_target="InvertDiagBlocksLowerTriangular" | custom-call | tf_op jit(solution)/shard_map/jit(cholesky)/cholesky | solution.py:14
  136.5 11.9 %cholesky.343 = f32[128,128]{1,0:T(8,128)S(1)} custom-call(f32[128,128]{1,0:T(8,128)S(1)} %convolution_subtract_fusion.25), custom_call_target="Cholesky" | custom-call | tf_op jit(solution)/shard_map/jit(cholesky)/cholesky | solution.py:14
  154.2 14.0 %while.2 = (s32[]{:T(128)}, f32[512,512]{1,0:T(8,128)}, s32[4,2]{0,1:T(2,128)S(1)}, f32[4,128,128]{2,1,0:T(8,128)}, s32[]{:T(128)}) while((s32[]{:T(128)}, f32[512,512]{1,0:T(8,128)}, s32[4,2]{0,1:T(2,128)S(1)}, f32[4,128,128]{2,1,0:T(8,128)}, s32[]{:T(128)}) %tuple.104), condition=%wide.while_cond, body=%wide.while_body.sunk | while | flops 2 | bytes 132205 | solution.py:15
  154.8 2.9 bitcast_dynamic-update-slice_fusion.4
  158.3 2.9 bitcast_dynamic-update-slice_fusion.4
  161.8 2.9 bitcast_dynamic-update-slice_fusion.4
  165.4 2.9 bitcast_dynamic-update-slice_fusion.4
  168.2 40.1 %custom-call.28 = f32[4,128,128]{1,2,0:T(8,128)S(1)} custom-call(f32[4,128,128]{2,1,0:T(8,128)} %get-tuple-element.13), custom_call_target="InvertDiagBlocksLowerTriangular" | custom-call | tf_op jit(solution)/shard_map/triangular_solve | solution.py:15
  209.1 1.4 fusion.41
  211.7 1.7 convolution_subtract_fusion.8
  213.4 1.9 constant_dynamic-update-slice_fusion.2
  215.3 1.6 convolution_subtract_fusion.7
  218.0 1.9 convolution_subtract_fusion.11
  220.9 1.9 convolution_subtract_fusion.1
  224.3 11.7 %cholesky.358 = f32[128,128]{1,0:T(8,128)S(1)} custom-call(f32[128,128]{1,0:T(8,128)S(1)} %cholesky.439), custom_call_target="Cholesky" | custom-call | tf_op jit(solution)/shard_map/jit(cholesky)/cholesky | solution.py:21
  236.2 10.2 %custom-call.36 = f32[1,128,128]{1,2,0:T(8,128)S(1)} custom-call(f32[1,128,128]{2,1,0:T(8,128)S(1)} %get-tuple-element.117), custom_call_target="InvertDiagBlocksLowerTriangular" | custom-call | tf_op jit(solution)/shard_map/jit(cholesky)/cholesky | solution.py:21
  246.4 1.3 fusion.56
  247.7 1.4 convolution_subtract_fusion.13
  249.3 11.7 %cholesky.377 = f32[128,128]{1,0:T(8,128)S(1)} custom-call(f32[128,128]{1,0:T(8,128)S(1)} %cholesky.443), custom_call_target="Cholesky" | custom-call | tf_op jit(solution)/shard_map/jit(cholesky)/cholesky | solution.py:21
  261.1 9.8 %custom-call.37 = f32[1,128,128]{1,2,0:T(8,128)S(1)} custom-call(f32[1,128,128]{2,1,0:T(8,128)S(1)} %get-tuple-element.114), custom_call_target="InvertDiagBlocksLowerTriangular" | custom-call | tf_op jit(solution)/shard_map/jit(cholesky)/cholesky | solution.py:21
  271.2 1.3 convolution_subtract_fusion.15
  272.5 11.7 %cholesky.398 = f32[128,128]{1,0:T(8,128)S(1)} custom-call(f32[128,128]{1,0:T(8,128)S(1)} %cholesky.448), custom_call_target="Cholesky" | custom-call | tf_op jit(solution)/shard_map/jit(cholesky)/cholesky | solution.py:21
  284.2 10.0 %custom-call.38 = f32[1,128,128]{1,2,0:T(8,128)S(1)} custom-call(f32[1,128,128]{2,1,0:T(8,128)S(1)} %get-tuple-element.111), custom_call_target="InvertDiagBlocksLowerTriangular" | custom-call | tf_op jit(solution)/shard_map/jit(cholesky)/cholesky | solution.py:21
  295.6 11.7 %cholesky.415 = f32[128,128]{1,0:T(8,128)S(1)} custom-call(f32[128,128]{1,0:T(8,128)S(1)} %convolution_subtract_fusion.24), custom_call_target="Cholesky" | custom-call | tf_op jit(solution)/shard_map/jit(cholesky)/cholesky | solution.py:21
  313.6 6.0 %fusion = (f32[1024,1024]{1,0:T(8,128)}, f32[1024,1024]{1,0:T(8,128)}) fusion(f32[512,1024]{1,0:T(8,128)} %select_dynamic-update-slice_fusion, f32[512,512]{1,0:T(8,128)S(1)} %get-tuple-element.49), kind=kLoop, calls=%fused_computation.7 | loop fusion | flops 5242880 | bytes 11534336 | tf_op jit(solution)/shard_map/triangular_solve | solution.py:28
  319.6 28.0 %while.3 = (s32[]{:T(128)}, f32[1024,1024]{1,0:T(8,128)}, s32[8,2]{0,1:T(2,128)S(1)}, f32[8,128,128]{2,1,0:T(8,128)}, s32[]{:T(128)}) while((s32[]{:T(128)}, f32[1024,1024]{1,0:T(8,128)}, s32[8,2]{0,1:T(2,128)S(1)}, f32[8,128,128]{2,1,0:T(8,128)}, s32[]{:T(128)}) %tuple.107), condition=%wide.while_cond.1, body=%wide.while_body.1.sunk | while | flops 2 | bytes 132205 | solution.py:28
  320.2 2.9 bitcast_dynamic-update-slice_fusion.5
  323.8 2.9 bitcast_dynamic-update-slice_fusion.5
  327.3 2.9 bitcast_dynamic-update-slice_fusion.5
  330.8 2.9 bitcast_dynamic-update-slice_fusion.5
  334.3 2.9 bitcast_dynamic-update-slice_fusion.5
  337.8 2.9 bitcast_dynamic-update-slice_fusion.5
  341.3 2.9 bitcast_dynamic-update-slice_fusion.5
  344.8 2.8 bitcast_dynamic-update-slice_fusion.5
  347.6 79.6 %custom-call.29 = f32[8,128,128]{1,2,0:T(8,128)S(1)} custom-call(f32[8,128,128]{2,1,0:T(8,128)} %get-tuple-element.21), custom_call_target="InvertDiagBlocksLowerTriangular" | custom-call | tf_op jit(solution)/shard_map/triangular_solve | solution.py:28
  427.3 1.4 constant_dynamic-update-slice_fusion.21
  428.7 1.6 convolution_subtract_fusion.6
  430.8 2.2 convolution_subtract_fusion.5
  433.4 2.4 convolution_subtract_fusion.10
  436.3 2.8 convolution_subtract_fusion.12
  439.5 3.2 convolution_subtract_fusion.4
  443.2 3.6 convolution_subtract_fusion.9
  447.2 4.5 convolution_subtract_fusion.3
  452.1 1.5 broadcast_select_fusion
  459.7 1.2 convolution_subtract_fusion.23
  461.9 1.3 convolution_subtract_fusion.22
  464.2 1.4 convolution_subtract_fusion.19
  466.6 1.5 convolution_subtract_fusion.18
  469.0 2.0 copy.46
  471.0 1.7 convolution_subtract_fusion.17
  473.7 1.3 constant_dynamic-slice_fusion.2
  475.0 1.6 constant_dynamic-slice_fusion.3
  476.6 5.2 convolution_subtract_fusion.2
  481.7 88.6 %all-reduce.4.cloned.1.call-done = f32[512,1024]{0,1:T(8,128)} async-done(((f32[512,1024]{0,1:T(8,128)}), f32[512,1024]{0,1:T(8,128)}) %all-reduce.4.cloned.1.call-update) | async-done | bytes 2097168 | tf_op jit(solution)/shard_map/psum | solution.py:9
  570.4 6.3 %convolution_subtract_fusion = f32[512,512]{1,0:T(8,128)} fusion(f32[512,512]{1,0:T(8,128)} %param.8, f32[512,1024]{0,1:T(8,128)S(1)} %convolution_dynamic-update-slice_fusion, f32[512,1024]{0,1:T(8,128)} %all-reduce.4.cloned.1.call-done), kind=kOutput, calls=%fused_computation.8 | convolution fusion | flops 3221487616 | bytes 6291456 | tf_op jit(solution)/shard_map/ik,jk->ij/dot_general | solution.py:41
  (109 shorter events, 38.8 us)
Async XLA Ops:
  7.2 58.6 %all-gather.2.cloned.1.call-start = ((), (), s32[]{:S(2)}) async-start(), calls=%async_computation | async-start | bytes 4325376 | tf_op jit(solution)/shard_map/all_gather | solution.py:35
  7.9 562.5 %all-reduce.4.cloned.1.call-start = ((), (), s32[]{:S(2)}) async-start(), calls=%async_computation.1 | async-start | bytes 4194304 | tf_op jit(solution)/shard_map/psum | solution.py:9
  208.3 0.7 copy-start.5
  210.4 0.9 copy-start.1
  211.7 5.2 copy-start.6
  223.3 1.0 copy-start
  430.3 3.1 copy-start.3
  453.6 1.0 copy-start.2
  469.0 7.5 %copy-start.4 = (f32[512,128]{1,0:T(8,128)S(1)}, f32[512,128]{1,0:T(8,128)}, u32[]{:S(2)}) copy-start(f32[512,128]{1,0:T(8,128)} %param.10) | copy-start | bytes 786436
Sparse Core Ops, SparseCore 0:
  10.5 55.2 all-gather.1
  453.8 116.5 all-reduce.3
where the time goes:
time: 594 us; the launch traced here: 584 us
  other arithmetic  290 us (49%)
  waiting for transfers between devices  118 us (20%)
  matrix products  73.2 us (12%)
  local copies, waits for them, and re-layouts  53.1 us (9%)
  blocking collectives  29.2 us (5%)
  between operations  20 us (3%)
    psum x1, waiting for transfers between devices, broadcast(): return lax.psum(block, axis)  88.6 us
    another operation x3, other arithmetic, solve_rows(): lax.linalg.triangular_solve(lead_lower, rows_in, left_side=False, lower=T...  85.6 us
    another operation x15, other arithmetic, factor(): second_diag = jnp.linalg.cholesky(schur_block)  79.5 us
    another operation x14, other arithmetic, factor(): first_diag = jnp.linalg.cholesky(matrix[:half_size, :half_size])  78.9 us
    another operation x36, local copies, waits for them, and re-layouts  42 us
    another operation x3, other arithmetic, factor(): lax.linalg.triangular_solve(first_diag, matrix[half_size:, :half_size], l...  41.4 us
    all_gather x1, blocking collectives, shards(): lax.all_gather(charge_lead, 'row', axis=0, tiled=True)  29.2 us
    all_gather x1, waiting for transfers between devices, shards(): lax.all_gather(lead_block, 'row', axis=0, tiled=True)  28.6 us
  transfers between devices with their start and end apart: 2, of which 2 were waited for; matrix products, arithmetic and copies ran while one was open for 5% of the time, Pallas kernels for 0%

commit v1 on v0

v1 whole, which is shorter than its diff:
```python
import collections
import jax
import jax.numpy as jnp
from jax import lax
from jax.experimental import pallas as pl
from jax.experimental.pallas import tpu as pltpu
from jax.sharding import PartitionSpec as P

F32, BF16 = jnp.float32, jnp.bfloat16
B = 128
BLOCKS = 8


def lane(x, i):
    return jnp.broadcast_to(x[:, i:i + 1], (8, B))


def sub(x, j):
    return jnp.broadcast_to(x[j:j + 1, :], (8, B))


def factor(rows, aug, upper, inverse):
    row_of = lax.broadcasted_iota(jnp.int32, (8, B), 0)
    lane_of = lax.broadcasted_iota(jnp.int32, (8, B), 1)
    n = len(rows)
    own = [lane(rows[0], i) for i in range(8)]
    for g in range(n):
        a, b = rows[g], aug[g]
        if g + 1 < n:
            below = [lane(rows[g + 1], 8 * g + i) for i in range(8)]
            after = [lane(rows[g + 1], 8 * g + 8 + i) for i in range(8)]
        dinv = None
        for j in range(8):
            heads = {i: sub(own[i], j) for i in range(j, 8)}
            r = 1.0 / heads[j]
            dinv = r if j == 0 else jnp.where(row_of == j, r, dinv)
            m = jnp.where(row_of > j, own[j] * r, 0.0)
            for i in range(j + 1, 8):
                own[i] = own[i] - m * heads[i]
            if j < 7:
                a = a - m * sub(a, j)
                b = b - m * sub(b, j)
            if g + 1 < n:
                mn = below[j] * r
                for i in range(j + 1, 8):
                    below[i] = below[i] - mn * heads[i]
                for i in range(8):
                    after[i] = after[i] - mn * sub(below[j], i)
            yield
        scale = jnp.sqrt(dinv)
        upper.append(jnp.where(lane_of >= row_of + 8 * g, a * scale, 0.0))
        inverse.append(b * scale)
        if g + 1 < n:
            za, zb = a * dinv, b * dinv
            for j in range(7, 0, -1):
                t = jnp.where(row_of < j, own[j] * dinv, 0.0)
                za = za - t * sub(za, j)
                zb = zb - t * sub(zb, j)
            sa = [sub(za, i) for i in range(8)]
            sb = [sub(zb, i) for i in range(8)]
            for h in range(g + 1, n):
                col = [lane(rows[h], 8 * g + i) for i in range(8)]
                pa = [col[i] * sa[i] for i in range(8)]
                pb = [col[i] * sb[i] for i in range(8)]
                rows[h] = rows[h] - (((pa[0] + pa[1]) + (pa[2] + pa[3])) + ((pa[4] + pa[5]) + (pa[6] + pa[7])))
                aug[h] = aug[h] - (((pb[0] + pb[1]) + (pb[2] + pb[3])) + ((pb[4] + pb[5]) + (pb[6] + pb[7])))
            own = after


def two(x):
    h = x.astype(BF16)
    return h, (x - h.astype(F32)).astype(BF16)


def three(x):
    h = x.astype(BF16)
    r = x - h.astype(F32)
    m = r.astype(BF16)
    return h, m, (r - m.astype(F32)).astype(BF16)


def left6(x):
    h, m, l = three(x)
    return jnp.concatenate([h, h, m, h, m, l], 1)


def right6(x, axis=0):
    h, m, l = three(x)
    return jnp.concatenate([h, m, h, l, m, h], axis)


def left3(x):
    h, l = two(x)
    return jnp.concatenate([h, l, h], 1)


def right3(x, axis=0):
    h, l = two(x)
    return jnp.concatenate([h, h, l], axis)


def mul(x, y):
    return jnp.dot(x, y, preferred_element_type=F32)


def mul_t(x, y):
    return lax.dot_general(x, y, (((1,), (1,)), ((), ())), preferred_element_type=F32)


def at(i):
    return slice(i * B, i * B + B)


class Plan:
    def __init__(self, s, z, c, t, r, rows):
        self.s, self.z, self.c, self.t, self.r = s, z, c, t, r
        self.rows = rows
        self.queue = collections.deque()

    def drain(self, count=None):
        while self.queue and (count is None or count > 0):
            self.queue.popleft()()
            if count is not None:
                count -= 1

    def step(self, k):
        s = self.s
        row_of = lax.broadcasted_iota(jnp.int32, (8, B), 0)
        lane_of = lax.broadcasted_iota(jnp.int32, (8, B), 1)
        rows = [s[k * B + 8 * g:k * B + 8 * g + 8, at(k)] for g in range(16)]
        aug = [jnp.where(lane_of == row_of + 8 * g, 1.0, 0.0).astype(F32) for g in range(16)]
        upper, inverse = [], []
        total = len(self.queue)
        done = 0
        for n, _ in enumerate(factor(rows, aug, upper, inverse)):
            due = min(total, (n + 1) * total // 112)
            self.drain(due - done)
            done = due
        self.drain()
        self.after(k, jnp.concatenate(upper, 0), jnp.concatenate(inverse, 0))

    def after(self, k, upper, w):
        s, z, c, t, r, half = self.s, self.z, self.c, self.t, self.r, self.rows
        add = self.queue.append
        wl = left6(w)
        wt = w.T
        wr = right6(wt)
        wr3 = right3(wt)
        last = BLOCKS - 1
        later = range(k + 1, BLOCKS)
        ql, pr, pr3 = {}, {}, {}

        def panel(j):
            p = mul(wl, right6(s[at(k), at(j)]))
            pr[j] = right6(p)
            pr3[j] = right3(p)

        def column(i):
            q = mul(left6(s[at(i), at(k)]), wr)
            s[at(i), at(k)] = q
            ql[i] = left6(q)

        def trail(i, j):
            s[at(i), at(j)] = s[at(i), at(j)] - mul(ql[i], pr[j])

        def diagonal():
            s[at(k), at(k)] = upper.T

        if k < last:
            panel(k + 1)
            column(k + 1)
            trail(k + 1, k + 1)
            for j in range(k + 2, BLOCKS):
                add(lambda j=j: panel(j))
                add(lambda j=j: column(j))
                if j == k + 2:
                    add(lambda j=j: trail(k + 1, j))
                    add(lambda j=j: trail(j, k + 1))
                    add(lambda j=j: trail(j, j))
            for i in later:
                for j in later:
                    if max(i, j) > k + 2:
                        add(lambda i=i, j=j: trail(i, j))
        add(diagonal)
        xs = {}
        ys = {}

        def solve(m):
            rows = slice(m * 256, m * 256 + 256)
            x = mul(left3(z[rows, at(k)]), wr3)
            z[rows, at(k)] = x
            xs[m] = left3(x)
            if m >= half // 256:
                xs[m, "r"] = right3(x, 1)

        def sweep(m, j, wide):
            rows = slice(m * 256, m * 256 + 256)
            cols = slice(j * B, (j + wide) * B)
            rhs = jnp.concatenate([pr3[j + i] for i in range(wide)], 1)
            z[rows, cols] = z[rows, cols] - mul(xs[m], rhs)

        def right():
            y = mul(left3(w), right3(c[at(k), :]))
            c[at(k), :] = y
            ys[0] = right3(y)

        def right_below(i):
            q = s[at(i), at(k)]
            c[at(i), :] = c[at(i), :] - mul(left3(q), ys[0])

        def slab(m, n):
            rows = slice(m * 256, m * 256 + 256)
            cols = slice(n * 256, n * 256 + 256)
            t[rows, cols] = t[rows, cols] - mul_t(xs[m], xs[n + half // 256, "r"])

        def rest(m):
            rows = slice(m * 256, m * 256 + 256)
            r[rows, :] = r[rows, :] - mul(xs[m], ys[0])

        parts = 2 * half // 256
        for m in range(parts):
            add(lambda m=m: solve(m))
        add(right)
        j = k + 1
        while j < BLOCKS:
            wide = 2 if j + 1 < BLOCKS else 1
            for m in range(parts):
                add(lambda m=m, j=j, wide=wide: sweep(m, j, wide))
            j += wide
        for i in later:
            add(lambda i=i: right_below(i))
        for m in range(half // 256):
            for n in range(t.shape[1] // 256):
                add(lambda m=m, n=n: slab(m, n))
        for m in range(half // 256):
            add(lambda m=m: rest(m))


def whole(s, z, c, t, r, rows):
    plan = Plan(s, z, c, t, r, rows)
    for k in range(BLOCKS):
        plan.step(k)
    plan.drain()


def kernel(lead, panel, far, charge, slab, rest, lead_out, panel_out, slab_out, charge_out, rest_out, s, z, c, sem, out_sem):
    half = panel.shape[0]
    here = [(lead, s), (panel, z.at[0:half]), (far, z.at[half:2 * half]), (charge, c), (slab, slab_out), (rest, rest_out)]
    copies = [pltpu.make_async_copy(a, b, sem.at[i]) for i, (a, b) in enumerate(here)]
    for copy in copies:
        copy.start()
    for copy in copies:
        copy.wait()
    whole(s, z, c, slab_out, rest_out, half)
    count = lead_out.shape[0]
    first = pl.multiple_of(lax.axis_index("row") * count, count)
    column = lax.broadcasted_iota(jnp.int32, lead_out.shape, 1)
    line = lax.broadcasted_iota(jnp.int32, lead_out.shape, 0) + first
    lead_out[...] = jnp.where(column <= line, s[pl.ds(first, count), :], 0.0)
    charge_out[...] = c[pl.ds(first, count), :]
    copy = pltpu.make_async_copy(z.at[0:half], panel_out, out_sem)
    copy.start()
    copy.wait()


def shards(lead_block, panel_block, trailing_slab, charge_lead, charge_rest):
    lead_whole = lax.all_gather(lead_block, "row", axis=0, tiled=True)
    charge_whole = lax.all_gather(charge_lead, "row", axis=0, tiled=True)
    mine = lax.axis_index("row") == lax.axis_index("col")
    far = lax.psum(jnp.where(mine, panel_block, 0.0), "row")
    vmem = pl.BlockSpec(memory_space=pltpu.VMEM)
    hbm = pl.BlockSpec(memory_space=pl.ANY)
    like = lambda a: jax.ShapeDtypeStruct(a.shape, F32)
    lead_mine, lower_panel, slab, solved, rest = pl.pallas_call(
        kernel,
        out_shape=[like(lead_block), like(panel_block), like(trailing_slab), like(charge_lead), like(charge_rest)],
        in_specs=[hbm] * 6,
        out_specs=[vmem, hbm, vmem, vmem, vmem],
        scratch_shapes=[
            pltpu.VMEM(lead_whole.shape, F32),
            pltpu.VMEM((2 * panel_block.shape[0], panel_block.shape[1]), F32),
            pltpu.VMEM(charge_whole.shape, F32),
            pltpu.SemaphoreType.DMA((6,)),
            pltpu.SemaphoreType.DMA,
        ],
        compiler_params=pltpu.CompilerParams(vmem_limit_bytes=56 * 2**20),
    )(lead_whole, panel_block, far, charge_whole, trailing_slab, charge_rest)
    return lead_mine, lower_panel, slab, solved, rest


def solution(mesh):
    placed = (P("row", None), P("row", None), P("row", "col"), P("row", "col"), P("row", "col"))
    return jax.shard_map(shards, mesh=mesh, in_specs=placed, out_specs=placed, check_vma=False)
```

time: 594 us -> 237 us (0.40); the launches traced: 584 us -> 237 us
  other arithmetic: 290 us -> 1.62 us
  matrix products: 73.2 us -> 0 us
  local copies, waits for them, and re-layouts: 53.1 us -> 0.01 us
  Pallas kernels: 0 us -> 42 us
  waiting for transfers between devices: 118 us -> 150 us
    another operation x35 -> x0, other arithmetic: 285 us -> none  [the longest x3 85.6 us: solve_rows(): lax.linalg.triangular_solve(lead_lower, rows_in, left_side=False, lower=T...]
    another operation x49 -> x0, matrix products: 59.9 us -> none  [the longest x15 24.7 us: solve_rows(): lax.linalg.triangular_solve(lead_lower, rows_in, left_side=False, lower=T...]
    another operation x49 -> x0, local copies, waits for them, and re-layouts: 42.6 us -> none
    pallas_call x0 -> x1, Pallas kernels: none -> 42 us  [shards(): pl.pallas_call(kernel, out_shape=[like(lead_block), like(panel_block), li...]
    all_gather x1, waiting for transfers between devices: 28.6 us -> 53.9 us  [shards(): lead_whole = lax.all_gather(lead_block, 'row', axis=0, tiled=True)]
    dot_general x3 -> x0, matrix products: 13.3 us -> none  [the longest x1 6.32 us: shards(): jnp.einsum('ik,jk->ij', lower_panel, far_lower, precision=lax.Precision.H...]
    psum x1, waiting for transfers between devices: 88.6 us -> 94.9 us  [shards(): far = lax.psum(jnp.where(mine, panel_block, 0.0), 'row')]
    unnamed x18 -> x2, local copies, waits for them, and re-layouts: 6.06 us -> 0.01 us
  transfers between devices with their start and end apart: 2 -> 2, of which waited for: 2 -> 2; matrix products, arithmetic and copies ran while one was open for 5% -> 0% of each run, Pallas kernels for 0% -> 0%
where the time goes in v1:
time: 237 us
  waiting for transfers between devices  150 us (63%)
  Pallas kernels  42 us (18%)
  blocking collectives  29.2 us (12%)
  between operations  14.1 us (6%)
    psum x1, waiting for transfers between devices, shards(): far = lax.psum(jnp.where(mine, panel_block, 0.0), 'row')  94.9 us
    all_gather x1, waiting for transfers between devices, shards(): lead_whole = lax.all_gather(lead_block, 'row', axis=0, tiled=True)  53.9 us
    pallas_call x1, Pallas kernels, shards(): pl.pallas_call(kernel, out_shape=[like(lead_block), like(panel_block), li...  42 us
    all_gather x1, blocking collectives, shards(): charge_whole = lax.all_gather(charge_lead, 'row', axis=0, tiled=True)  29.2 us
  transfers between devices with their start and end apart: 2, of which 2 were waited for; matrix products, arithmetic and copies ran while one was open for 0% of the time, Pallas kernels for 0%

profile of v1, /device:TPU:1, one launch (start us, length us, event | category | flops | bytes accessed | tf_op | source)
XLA Modules:
  0.0 236.5 jit_solution(59036723152422877)
XLA Ops:
  7.2 0.0 all-reduce.2.cloned.1.call-start
  7.2 1.6 broadcast_select_fusion
  8.8 0.0 copy-start
  8.8 0.0 all-reduce.2.cloned.1.call-update
  8.9 0.0 all-gather.2.cloned.1.call-start
  8.9 0.7 all-gather.2.cloned.1.call-update
  9.6 0.0 copy-done
  9.6 29.2 %all_gather.7.charge = f32[1024,128]{1,0:T(8,128)} all-gather(f32[32,128]{1,0:T(8,128)S(1)} %copy-done), channel_id=1, replica_groups=mesh['row'=32,'col'=8] {'row'}, dimensions={0}, use_global_device_ids=true | all-gather | bytes 540672 | tf_op jit(solution)/shard_map/all_gather | solution.py:268
  38.8 94.9 %all-reduce.2.cloned.1.call-done.far = f32[512,1024]{1,0:T(8,128)} async-done(((f32[512,1024]{1,0:T(8,128)}), f32[512,1024]{1,0:T(8,128)}) %all-reduce.2.cloned.1.call-update) | async-done | bytes 2097168 | tf_op jit(solution)/shard_map/psum | solution.py:270
  133.8 53.9 %all-gather.2.cloned.1.call-done.lead = f32[1024,1024]{1,0:T(8,128)} async-done(((f32[32,1024]{1,0:T(8,128)}), f32[1024,1024]{1,0:T(8,128)}) %all-gather.2.cloned.1.call-update) | async-done | bytes 4194320 | tf_op jit(solution)/shard_map/all_gather | solution.py:267
  187.7 42.0 %shard_map.92 = (f32[32,1024]{1,0:T(8,128)}, f32[512,1024]{1,0:T(8,128)}, f32[512,512]{1,0:T(8,128)}, f32[32,128]{1,0:T(8,128)}, f32[512,128]{1,0:T(8,128)}) custom-call(f32[1024,1024]{1,0:T(8,128)} %all-gather.2.cloned.1.call-done.lead, f32[512,1024]{1,0:T(8,128)} %panel.1, f32[512,1024]{1,0:T(8,128)} %all-reduce.2.cloned.1.call-done.far, ...), custom_call_target="tpu_custom_call" | custom-call | tf_op jit(solution)/shard_map/pallas_call | solution.py:274
Async XLA Ops:
  7.2 126.6 %all-reduce.2.cloned.1.call-start = ((), (), s32[]{:S(2)}) async-start(), calls=%async_computation.1 | async-start | bytes 4194304 | tf_op jit(solution)/shard_map/psum | solution.py:270
  8.8 0.8 copy-start
  8.9 178.8 %all-gather.2.cloned.1.call-start = ((), (), s32[]{:S(2)}) async-start(), calls=%async_computation | async-start | bytes 4325376 | tf_op jit(solution)/shard_map/all_gather | solution.py:267
Sparse Core Ops, SparseCore 0:
  11.8 121.9 all-reduce.1
  136.3 51.2 all-gather.1

commit v2 on v1

--- a/solution.py
+++ b/solution.py
@@ -263,11 +263,163 @@
     copy.wait()
 
 
+MESH = pl.DeviceIdType.MESH
+
+
+def gather(lead, panel, charge, lead_all, far_all, charge_all, send_sem, recv_sem, far_send, far_recv, spread_sem, local_sem):
+    row, col = lax.axis_index("row"), lax.axis_index("col")
+    core, chip = row % 2, row // 2
+    x, y = chip % 4, chip // 4
+    u = x * (1 - core) + y * core
+    v = y * (1 - core) + x * core
+
+    def place(a, b, kind=core):
+        return ((b * 4 + a) * (1 - kind) + (a * 4 + b) * kind) * 2 + kind
+
+    def ring(i):
+        return (i + 4) % 4
+
+    sibling = row + 1 - 2 * core
+    devices = lead_all.shape[0] // lead.shape[0]
+    rows, piece, line = lead.shape[0], far_all.shape[0] // devices, charge.shape[0]
+
+    barrier = pltpu.get_barrier_semaphore()
+
+    def greet(i, carry):
+        pl.semaphore_signal(barrier, inc=1, device_id=((row + i) % devices, col), device_id_type=MESH)
+        return carry
+
+    lax.fori_loop(1, devices, greet, 0)
+    pl.semaphore_wait(barrier, devices - 1)
+
+    def cut(ref, owner, size):
+        return ref.at[pl.ds(pl.multiple_of(owner * size, size), size)]
+
+    def spread(other):
+        return pltpu.make_async_remote_copy(
+            src_ref=cut(panel, other, piece), dst_ref=cut(far_all, other, piece),
+            send_sem=spread_sem.at[other], recv_sem=far_recv.at[other],
+            device_id=(other, col), device_id_type=MESH)
+
+    mine = [pltpu.make_async_copy(lead, cut(lead_all, row, rows), local_sem.at[0]),
+            pltpu.make_async_copy(charge, cut(charge_all, row, line), local_sem.at[1])]
+
+    started = ([], [], [])
+    arrays = [(lead, lead_all, rows, send_sem.at[0], recv_sem.at[0]),
+              (charge, charge_all, line, send_sem.at[1], recv_sem.at[1]),
+              (None, far_all, piece, far_send, far_recv)]
+    kinds = ((0, 1), (2,))
+
+    def send(kind, owner, target, own=False):
+        for n in kinds[kind]:
+            source, ref, size, out, into = arrays[n]
+            copy = pltpu.make_async_remote_copy(
+                src_ref=source if own and source is not None else cut(ref, owner, size),
+                dst_ref=cut(ref, owner, size),
+                send_sem=out.at[len(started[n])], recv_sem=into.at[owner],
+                device_id=(target, col), device_id_type=MESH)
+            copy.start()
+            started[n].append(copy)
+
+    def arrived(kind, owner):
+        for n in kinds[kind]:
+            _, ref, size, _, into = arrays[n]
+            pltpu.make_async_copy(cut(ref, owner, size), cut(ref, owner, size), into.at[owner]).wait()
+
+    def across(kind, owner, own=False):
+        send(kind, owner, place(u, ring(v + 1)), own)
+        send(kind, owner, place(u, ring(v - 1)), own)
+        send(kind, owner, sibling, own)
+
+    def own(kind):
+        send(kind, row, place(ring(u + 1), v), True)
+        send(kind, row, place(ring(u - 1), v), True)
+        across(kind, row, True)
+
+    def first(kind):
+        e = (1 - 2 * kind) * (2 * (u % 2) - 1)
+        owner = place(ring(u - e), v)
+        arrived(kind, owner)
+        send(kind, owner, place(ring(u + e), v))
+        across(kind, owner)
+        for a in (ring(u + e), ring(u + 2)):
+            owner = place(a, v)
+            arrived(kind, owner)
+            across(kind, owner)
+
+    def second(kind):
+        f = (1 - 2 * kind) * (2 * (v % 2) - 1)
+        order = [u, ring(u + 1), ring(u - 1), ring(u + 2)]
+        for a in order:
+            owner = place(a, ring(v - f))
+            arrived(kind, owner)
+            send(kind, owner, place(u, ring(v + f)))
+            send(kind, owner, sibling)
+            owner = place(a, ring(v + f))
+            arrived(kind, owner)
+            send(kind, owner, sibling)
+        for a in order:
+            owner = place(a, ring(v + 2))
+            arrived(kind, owner)
+            send(kind, owner, sibling)
+
+    own(0)
+    for copy in mine:
+        copy.start()
+
+    @pl.when(row == col)
+    def _():
+        def go(i, carry):
+            spread((row + i) % devices).start()
+            return carry
+
+        lax.fori_loop(1, devices, go, 0)
+        pltpu.make_async_copy(cut(panel, row, piece), cut(far_all, row, piece), far_recv.at[row]).start()
+
+    first(0)
+    arrived(1, row)
+    own(1)
+    second(0)
+    first(1)
+    second(1)
+    for kind in (0, 1):
+        for a in range(4):
+            for b in range(4):
+                arrived(kind, place(a, b, 1 - core))
+    for copy in mine:
+        copy.wait()
+    for group in started:
+        for copy in group:
+            copy.wait_send()
+
+    @pl.when(row == col)
+    def _():
+        def end(i, carry):
+            spread((row + i) % devices).wait_send()
+            return carry
+
+        lax.fori_loop(1, devices, end, 0)
+
+
+def gathered(lead_block, panel_block, charge_lead):
+    devices = lax.axis_size("row")
+    vmem = pl.BlockSpec(memory_space=pltpu.VMEM)
+    hbm = pl.BlockSpec(memory_space=pl.ANY)
+    tall = lambda a: jax.ShapeDtypeStruct((a.shape[0] * devices, a.shape[1]), F32)
+    dma = pltpu.SemaphoreType.DMA
+    return pl.pallas_call(
+        gather,
+        out_shape=[tall(lead_block), jax.ShapeDtypeStruct(panel_block.shape, F32), tall(charge_lead)],
+        in_specs=[hbm] * 3,
+        out_specs=[vmem] * 3,
+        scratch_shapes=[dma((2, devices - 1)), dma((2, devices)), dma((devices - 1,)), dma((devices,)),
+                        dma((devices,)), dma((2,))],
+        compiler_params=pltpu.CompilerParams(collective_id=0, has_side_effects=True, vmem_limit_bytes=20 * 2**20),
+    )(lead_block, panel_block, charge_lead)
+
+
 def shards(lead_block, panel_block, trailing_slab, charge_lead, charge_rest):
-    lead_whole = lax.all_gather(lead_block, "row", axis=0, tiled=True)
-    charge_whole = lax.all_gather(charge_lead, "row", axis=0, tiled=True)
-    mine = lax.axis_index("row") == lax.axis_index("col")
-    far = lax.psum(jnp.where(mine, panel_block, 0.0), "row")
+    lead_whole, far, charge_whole = gathered(lead_block, panel_block, charge_lead)
     vmem = pl.BlockSpec(memory_space=pltpu.VMEM)
     hbm = pl.BlockSpec(memory_space=pl.ANY)
     like = lambda a: jax.ShapeDtypeStruct(a.shape, F32)

time: 237 us -> 102 us (0.43)
  the two profiles are of different devices: /device:TPU:1 before, /device:TPU:139 now
where the time goes in v2:
time: 102 us
  Pallas kernels  93.5 us (92%)
  local copies, waits for them, and re-layouts  7.27 us (7%)
    pallas_call x1, Pallas kernels, gathered(): pl.pallas_call(gather, out_shape=[tall(lead_block), jax.ShapeDtypeStruct(...  51.5 us
    pallas_call x1, Pallas kernels, shards(): pl.pallas_call(kernel, out_shape=[like(lead_block), like(panel_block), li...  42 us
    unnamed x12, local copies, waits for them, and re-layouts  7.27 us

profile of v2, /device:TPU:139, one launch (start us, length us, event | category | flops | bytes accessed | tf_op | source)
XLA Modules:
  0.0 101.6 jit_solution(15145763737726237004)
XLA Ops:
  0.6 0.0 copy-start
  0.6 1.6 %copy-done = f32[512,1024]{1,0:T(8,128)S(1)} copy-done((f32[512,1024]{1,0:T(8,128)S(1)}, f32[512,1024]{1,0:T(8,128)}, u32[]{:S(2)}) %copy-start) | copy-done | bytes 2097176
  2.2 0.0 copy-start.4
  2.2 0.9 copy-done.4
  3.1 0.0 copy-start.5
  3.1 0.7 copy-done.5
  3.8 51.5 %shard_map.92 = (f32[1024,1024]{1,0:T(8,128)S(1)}, f32[512,1024]{1,0:T(8,128)S(1)}, f32[1024,128]{1,0:T(8,128)S(1)}) custom-call(f32[32,1024]{1,0:T(8,128)S(1)} %copy-done.4, f32[512,1024]{1,0:T(8,128)S(1)} %copy-done, f32[32,128]{1,0:T(8,128)S(1)} %copy-done.5), custom_call_target="tpu_custom_call" | custom-call | tf_op jit(solution)/shard_map/pallas_call | solution.py:410
  55.3 0.0 copy-start.1
  55.3 1.9 %copy-done.1 = f32[1024,1024]{1,0:T(8,128)} copy-done((f32[1024,1024]{1,0:T(8,128)}, f32[1024,1024]{1,0:T(8,128)S(1)}, u32[]{:S(2)}) %copy-start.1) | copy-done | bytes 4194328
  57.3 0.0 copy-start.2
  57.3 1.3 %copy-done.2 = f32[512,1024]{1,0:T(8,128)} copy-done((f32[512,1024]{1,0:T(8,128)}, f32[512,1024]{1,0:T(8,128)S(1)}, u32[]{:S(2)}) %copy-start.2) | copy-done | bytes 2097176
  58.6 0.0 copy-start.3
  58.6 0.8 copy-done.3
  59.4 42.0 %shard_map.93 = (f32[32,1024]{1,0:T(8,128)}, f32[512,1024]{1,0:T(8,128)}, f32[512,512]{1,0:T(8,128)}, f32[32,128]{1,0:T(8,128)}, f32[512,128]{1,0:T(8,128)}) custom-call(f32[1024,1024]{1,0:T(8,128)} %copy-done.1, f32[512,1024]{1,0:T(8,128)} %panel.3, f32[512,1024]{1,0:T(8,128)} %copy-done.2, f32[1024,128]{1,0:T(8,128)} %copy-done.3, f32[512,512]{1,0:T(8,128)} %slab.1, ...), custom_call_target="tpu_custom_call" | custom-call | tf_op jit(solution)/shard_map/pallas_call | solution.py:426
Async XLA Ops:
  0.6 1.6 %copy-start = (f32[512,1024]{1,0:T(8,128)S(1)}, f32[512,1024]{1,0:T(8,128)}, u32[]{:S(2)}) copy-start(f32[512,1024]{1,0:T(8,128)} %panel.3) | copy-start | bytes 6291460
  2.2 0.9 copy-start.4
  3.1 0.7 copy-start.5
  55.3 1.9 %copy-start.1 = (f32[1024,1024]{1,0:T(8,128)}, f32[1024,1024]{1,0:T(8,128)S(1)}, u32[]{:S(2)}) copy-start(f32[1024,1024]{1,0:T(8,128)S(1)} %get-tuple-element.8.lead) | copy-start | bytes 12582916
  57.3 1.3 %copy-start.2 = (f32[512,1024]{1,0:T(8,128)}, f32[512,1024]{1,0:T(8,128)S(1)}, u32[]{:S(2)}) copy-start(f32[512,1024]{1,0:T(8,128)S(1)} %get-tuple-element.9.far) | copy-start | bytes 6291460
  58.6 0.8 copy-start.3

commit v3 on v2

v3 whole, which is shorter than its diff:
```python
import collections
import jax
import jax.numpy as jnp
from jax import lax
from jax.experimental import pallas as pl
from jax.experimental.pallas import tpu as pltpu
from jax.sharding import PartitionSpec as P

F32, BF16 = jnp.float32, jnp.bfloat16
B = 128
BLOCKS = 8


def lane(x, i):
    return jnp.broadcast_to(x[:, i:i + 1], (8, B))


def sub(x, j):
    return jnp.broadcast_to(x[j:j + 1, :], (8, B))


def factor(rows, upper, inverse):
    row_of = lax.broadcasted_iota(jnp.int32, (8, B), 0)
    lane_of = lax.broadcasted_iota(jnp.int32, (8, B), 1)
    n = len(rows)
    own = [lane(rows[0], i) for i in range(8)]
    for g in range(n):
        here = (lane_of >= 8 * g) & (lane_of < 8 * g + 8)
        unit = jnp.where(lane_of == row_of + 8 * g, 1.0, 0.0)
        a = jnp.where(here, unit, rows[g])
        if g + 1 < n:
            below = [lane(rows[g + 1], 8 * g + i) for i in range(8)]
            after = [lane(rows[g + 1], 8 * g + 8 + i) for i in range(8)]
        dinv = None
        for j in range(8):
            heads = {i: sub(own[i], j) for i in range(j, 8)}
            r = 1.0 / heads[j]
            dinv = r if j == 0 else jnp.where(row_of == j, r, dinv)
            m = jnp.where(row_of > j, own[j] * r, 0.0)
            for i in range(j + 1, 8):
                own[i] = own[i] - m * heads[i]
            if j < 7:
                a = a - m * sub(a, j)
            if g + 1 < n:
                mn = below[j] * r
                for i in range(j + 1, 8):
                    below[i] = below[i] - mn * heads[i]
                for i in range(8):
                    after[i] = after[i] - mn * sub(below[j], i)
            yield
        scale = jnp.sqrt(dinv)
        corner = own[0]
        for i in range(1, 8):
            corner = jnp.where(lane_of == 8 * g + i, own[i], corner)
        corner = jnp.where(lane_of >= row_of + 8 * g, corner, 0.0)
        upper.append(jnp.where(lane_of < 8 * g + 8, jnp.where(here, corner, 0.0), a) * scale)
        inverse.append(jnp.where(lane_of < 8 * g + 8, a, 0.0) * scale)
        if g + 1 < n:
            z = a * dinv
            for j in range(7, 0, -1):
                t = jnp.where(row_of < j, own[j] * dinv, 0.0)
                z = z - t * sub(z, j)
            s = [sub(z, i) for i in range(8)]
            for h in range(g + 1, n):
                p = [lane(rows[h], 8 * g + i) * s[i] for i in range(8)]
                rows[h] = jnp.where(here, 0.0, rows[h]) - (
                    ((p[0] + p[1]) + (p[2] + p[3])) + ((p[4] + p[5]) + (p[6] + p[7])))
            own = after


def two(x):
    h = x.astype(BF16)
    return h, (x - h.astype(F32)).astype(BF16)


def three(x):
    h = x.astype(BF16)
    r = x - h.astype(F32)
    m = r.astype(BF16)
    return h, m, (r - m.astype(F32)).astype(BF16)


def left6(x):
    h, m, l = three(x)
    return jnp.concatenate([h, h, m, h, m, l], 1)


def right6(x, axis=0):
    h, m, l = three(x)
    return jnp.concatenate([h, m, h, l, m, h], axis)


def left4(x):
    h, l = two(x)
    return jnp.concatenate([h, l, h, l], 1)


def right4(x, axis=0):
    h, l = two(x)
    return jnp.concatenate([h, h, l, l], axis)


def parts(count):
    odd = count % 2
    lefts = [(n, p) for n in range(count - odd) for p in (0, 1, 0)]
    rights = [(n, p) for n in range(count - odd) for p in (0, 0, 1)]
    if odd:
        lefts += [(count - 1, p) for p in (0, 1, 0, 1)]
        rights += [(count - 1, p) for p in (0, 0, 1, 1)]
    return lefts, rights


def mul(x, y):
    return jnp.dot(x, y, preferred_element_type=F32)


def mul_t(x, y):
    return lax.dot_general(x, y, (((1,), (1,)), ((), ())), preferred_element_type=F32)


def at(i):
    return slice(i * B, i * B + B)


class Plan:
    def __init__(self, s, z, c, t, r, xs, us, ys, rows, ready, leave):
        self.s, self.z, self.c, self.t, self.r = s, z, c, t, r
        self.xs, self.us, self.ys = xs, us, ys
        self.rows, self.ready, self.leave = rows, ready, leave
        self.queue = collections.deque()

    def drain(self, count=None):
        while self.queue and (count is None or count > 0):
            self.queue.popleft()()
            if count is not None:
                count -= 1

    def step(self, k):
        s = self.s
        rows = [s[k * B + 8 * g:k * B + 8 * g + 8, at(k)] for g in range(16)]
        upper, inverse = [], []
        total = len(self.queue)
        done = 0
        for n, _ in enumerate(factor(rows, upper, inverse)):
            due = min(total, (n + 1) * total // 124)
            self.drain(due - done)
            done = due
        self.drain()
        self.ready(k)
        self.after(k, jnp.concatenate(upper, 0), jnp.concatenate(inverse, 0))

    def rights_of(self, k, first, count, cols):
        _, rights = parts(count)
        return jnp.concatenate([self.us[p, at(first + n), cols] for n, p in rights], 0)

    def lefts_of(self, rows, first, count):
        lefts, _ = parts(count)
        return jnp.concatenate([self.xs[p, rows, at(first + n)] for n, p in lefts], 1)

    def after(self, k, upper, w):
        s, z, c, t, r, half = self.s, self.z, self.c, self.t, self.r, self.rows
        xs, us, ys = self.xs, self.us, self.ys
        add = self.queue.append
        wl = left6(w)
        w4 = right4(w, 1)
        last = BLOCKS - 1
        ql, pr = {}, {}

        def panel(j):
            p = mul(wl, right6(s[at(k), at(j)]))
            h, m, l = three(p)
            pr[j] = jnp.concatenate([h, m, h, l, m, h], 0)
            us[0, at(k), at(j)] = h
            us[1, at(k), at(j)] = m
            q = p.T
            s[at(j), at(k)] = q
            ql[j] = left6(q)

        def trail(i, j):
            s[at(i), at(j)] = s[at(i), at(j)] - mul(ql[i], pr[j])

        def diagonal():
            s[at(k), at(k)] = upper.T

        def solve(m):
            rows = slice(m * 256, m * 256 + 256)
            x = mul_t(left4(z[rows, at(k)]), w4)
            z[rows, at(k)] = x
            h, l = two(x)
            xs[0, rows, at(k)] = h
            xs[1, rows, at(k)] = l

        def build(m):
            rows = slice(m * 256, m * 256 + 256)
            z[rows, at(k + 1)] = z[rows, at(k + 1)] - mul(
                self.lefts_of(rows, 0, k + 1), self.rights_of(k, 0, k + 1, at(k + 1)))

        def right():
            y = mul(left4(w), right4(c[at(k), :]))
            c[at(k), :] = y
            h, l = two(y)
            ys[0, at(k), :] = h
            ys[1, at(k), :] = l

        def right_below(i):
            h, l = ys[0, at(k), :], ys[1, at(k), :]
            c[at(i), :] = c[at(i), :] - mul(left4(s[at(i), at(k)]), jnp.concatenate([h, h, l, l], 0))

        def slab(m, n, first, count):
            rows = slice(m * 256, m * 256 + 256)
            cols = slice(n * 256, n * 256 + 256)
            lefts, rights = parts(count)
            far = slice(half + n * 256, half + n * 256 + 256)
            x = jnp.concatenate([xs[p, far, at(first + i)] for i, p in rights], 1)
            t[rows, cols] = t[rows, cols] - mul_t(self.lefts_of(rows, first, count), x)

        def rest(m, first, count):
            rows = slice(m * 256, m * 256 + 256)
            _, rights = parts(count)
            y = jnp.concatenate([ys[p, at(first + n), :] for n, p in rights], 0)
            r[rows, :] = r[rows, :] - mul(self.lefts_of(rows, first, count), y)

        if k < last:
            panel(k + 1)
            trail(k + 1, k + 1)
            for j in range(k + 2, BLOCKS):
                add(lambda j=j: panel(j))
            for j in range(k + 2, BLOCKS):
                add(lambda j=j: trail(k + 1, j))
        for m in range(2 * half // 256):
            add(lambda m=m: solve(m))
        add(lambda: self.leave(k))
        if k < last:
            for i in range(k + 2, BLOCKS):
                for j in range(i, BLOCKS):
                    add(lambda i=i, j=j: trail(i, j))
        add(right)
        if k < last:
            for m in range(2 * half // 256):
                add(lambda m=m: build(m))
        add(diagonal)
        for i in range(k + 1, BLOCKS):
            add(lambda i=i: right_below(i))
        groups = {1: (0, 2), 3: (2, 2), 5: (4, 2), 6: (6, 1), 7: (7, 1)}
        if k in groups:
            first, count = groups[k]
            for m in range(half // 256):
                for n in range(t.shape[1] // 256):
                    add(lambda m=m, n=n: slab(m, n, first, count))
            for m in range(half // 256):
                add(lambda m=m: rest(m, first, count))


def whole(s, z, c, t, r, xs, us, ys, rows, ready, leave):
    plan = Plan(s, z, c, t, r, xs, us, ys, rows, ready, leave)
    for k in range(BLOCKS):
        plan.step(k)
    plan.drain()


def kernel(lead, panel, far, charge, slab, rest, lead_out, panel_out, slab_out, charge_out, rest_out,
           s, z, c, xs, us, ys, sem, out_sem):
    half = panel.shape[0]
    here = [(lead.at[0:B], s.at[0:B]), (lead.at[B:], s.at[B:]), (panel, z.at[0:half]), (far, z.at[half:2 * half]),
            (charge, c), (slab, slab_out), (rest, rest_out)]
    copies = [pltpu.make_async_copy(a, b, sem.at[i]) for i, (a, b) in enumerate(here)]
    for copy in copies:
        copy.start()
    copies[0].wait()
    leaving = []

    def ready(k):
        if k == 0:
            for copy in copies[1:]:
                copy.wait()

    def leave(k):
        copy = pltpu.make_async_copy(z.at[0:half, at(k)], panel_out.at[:, at(k)], out_sem.at[k])
        copy.start()
        leaving.append(copy)

    whole(s, z, c, slab_out, rest_out, xs, us, ys, half, ready, leave)
    count = lead_out.shape[0]
    first = pl.multiple_of(lax.axis_index("row") * count, count)
    column = lax.broadcasted_iota(jnp.int32, lead_out.shape, 1)
    line = lax.broadcasted_iota(jnp.int32, lead_out.shape, 0) + first
    lead_out[...] = jnp.where(column <= line, s[pl.ds(first, count), :], 0.0)
    charge_out[...] = c[pl.ds(first, count), :]
    for copy in leaving:
        copy.wait()


MESH = pl.DeviceIdType.MESH


def gather(lead, panel, charge, lead_all, far_all, charge_all, send_sem, recv_sem, far_send, far_recv, spread_sem, local_sem):
    row, col = lax.axis_index("row"), lax.axis_index("col")
    planes = lax.axis_size("col")
    core, chip = row % 2, row // 2
    x, y = chip % 4, chip // 4
    u = x * (1 - core) + y * core
    v = y * (1 - core) + x * core

    def place(a, b, kind=core):
        return ((b * 4 + a) * (1 - kind) + (a * 4 + b) * kind) * 2 + kind

    def ring(i):
        return (i + 4) % 4

    sibling = row + 1 - 2 * core
    devices = lead_all.shape[0] // lead.shape[0]
    rows, piece, line = lead.shape[0], far_all.shape[0] // devices, charge.shape[0]

    barrier = pltpu.get_barrier_semaphore()

    share = devices // planes
    source = (col, row // share)
    near = [(place(ring(u + n), v), col) for n in (1, 2, 3)] + [(place(u, ring(v + n)), col) for n in (1, 2, 3)] + [(sibling, col)]
    for other in near:
        pl.semaphore_signal(barrier, inc=1, device_id=other, device_id_type=MESH)
    alone = (row == source[0]) & (col == source[1])

    @pl.when(jnp.logical_not(alone))
    def _():
        pl.semaphore_signal(barrier, inc=1, device_id=source, device_id_type=MESH)

    feeds = row < planes
    peers = jnp.where(feeds, len(near) + share, len(near)) - jnp.where(alone, 1, 0)
    pl.semaphore_wait(barrier, peers)

    def cut(ref, owner, size):
        return ref.at[pl.ds(pl.multiple_of(owner * size, size), size)]

    def spread(other, n):
        return pltpu.make_async_remote_copy(
            src_ref=cut(panel, other, piece), dst_ref=cut(far_all, other, piece),
            send_sem=spread_sem.at[n], recv_sem=far_recv.at[other],
            device_id=(other, row), device_id_type=MESH)

    mine = [pltpu.make_async_copy(lead, cut(lead_all, row, rows), local_sem.at[0]),
            pltpu.make_async_copy(charge, cut(charge_all, row, line), local_sem.at[1])]

    started = ([], [], [])
    arrays = [(lead, lead_all, rows, send_sem.at[0], recv_sem.at[0]),
              (charge, charge_all, line, send_sem.at[1], recv_sem.at[1]),
              (None, far_all, piece, far_send, far_recv)]
    kinds = ((0, 1), (2,))

    def send(kind, owner, target, own=False):
        for n in kinds[kind]:
            source, ref, size, out, into = arrays[n]
            copy = pltpu.make_async_remote_copy(
                src_ref=source if own and source is not None else cut(ref, owner, size),
                dst_ref=cut(ref, owner, size),
                send_sem=out.at[len(started[n])], recv_sem=into.at[owner],
                device_id=(target, col), device_id_type=MESH)
            copy.start()
            started[n].append(copy)

    def arrived(kind, owner):
        for n in kinds[kind]:
            _, ref, size, _, into = arrays[n]
            pltpu.make_async_copy(cut(ref, owner, size), cut(ref, owner, size), into.at[owner]).wait()

    def across(kind, owner, own=False):
        send(kind, owner, place(u, ring(v + 1)), own)
        send(kind, owner, place(u, ring(v - 1)), own)
        send(kind, owner, place(u, ring(v + 2)), own)
        send(kind, owner, sibling, own)

    def own(kind):
        send(kind, row, place(ring(u + 1), v), True)
        send(kind, row, place(ring(u - 1), v), True)
        send(kind, row, place(ring(u + 2), v), True)
        across(kind, row, True)

    def first(kind):
        e = (1 - 2 * kind) * (2 * (u % 2) - 1)
        owner = place(ring(u - e), v)
        arrived(kind, owner)
        across(kind, owner)
        for a in (ring(u + e), ring(u + 2)):
            owner = place(a, v)
            arrived(kind, owner)
            across(kind, owner)

    def second(kind):
        f = (1 - 2 * kind) * (2 * (v % 2) - 1)
        order = [u, ring(u + 1), ring(u - 1), ring(u + 2)]
        for a in order:
            owner = place(a, ring(v - f))
            arrived(kind, owner)
            send(kind, owner, sibling)
            owner = place(a, ring(v + f))
            arrived(kind, owner)
            send(kind, owner, sibling)
        for a in order:
            owner = place(a, ring(v + 2))
            arrived(kind, owner)
            send(kind, owner, sibling)

    own(0)
    for copy in mine:
        copy.start()

    for n in range(devices // lax.axis_size("col")):
        target = col * share + n

        @pl.when(feeds & ((target != row) | (row != col)))
        def _():
            spread(target, n).start()

    @pl.when(alone)
    def _():
        pltpu.make_async_copy(cut(panel, row, piece), cut(far_all, row, piece), far_recv.at[row]).start()

    first(0)
    arrived(1, row)
    own(1)
    second(0)
    first(1)
    second(1)
    for kind in (0, 1):
        for a in range(4):
            for b in range(4):
                arrived(kind, place(a, b, 1 - core))
    for copy in mine:
        copy.wait()
    for group in started:
        for copy in group:
            copy.wait_send()

    for n in range(devices // lax.axis_size("col")):
        target = col * share + n

        @pl.when(feeds & ((target != row) | (row != col)))
        def _():
            spread(target, n).wait_send()


def gathered(lead_block, panel_block, charge_lead):
    devices = lax.axis_size("row")
    vmem = pl.BlockSpec(memory_space=pltpu.VMEM)
    hbm = pl.BlockSpec(memory_space=pl.ANY)
    tall = lambda a: jax.ShapeDtypeStruct((a.shape[0] * devices, a.shape[1]), F32)
    dma = pltpu.SemaphoreType.DMA
    return pl.pallas_call(
        gather,
        out_shape=[tall(lead_block), jax.ShapeDtypeStruct(panel_block.shape, F32), tall(charge_lead)],
        in_specs=[hbm] * 3,
        out_specs=[hbm] * 3,
        scratch_shapes=[dma((2, devices - 1)), dma((2, devices)), dma((devices - 1,)), dma((devices,)),
                        dma((devices,)), dma((2,))],
        compiler_params=pltpu.CompilerParams(collective_id=0, has_side_effects=True, vmem_limit_bytes=60 * 2**20),
    )(lead_block, panel_block, charge_lead)


def shards(lead_block, panel_block, trailing_slab, charge_lead, charge_rest):
    lead_whole, far, charge_whole = gathered(lead_block, panel_block, charge_lead)
    vmem = pl.BlockSpec(memory_space=pltpu.VMEM)
    hbm = pl.BlockSpec(memory_space=pl.ANY)
    like = lambda a: jax.ShapeDtypeStruct(a.shape, F32)
    half, width = panel_block.shape
    return tuple(pl.pallas_call(
        kernel,
        out_shape=[like(lead_block), like(panel_block), like(trailing_slab), like(charge_lead), like(charge_rest)],
        in_specs=[hbm] * 6,
        out_specs=[vmem, hbm, vmem, vmem, vmem],
        scratch_shapes=[
            pltpu.VMEM(lead_whole.shape, F32),
            pltpu.VMEM((2 * half, width), F32),
            pltpu.VMEM(charge_whole.shape, F32),
            pltpu.VMEM((2, 2 * half, width), BF16),
            pltpu.VMEM((2,) + lead_whole.shape, BF16),
            pltpu.VMEM((2,) + charge_whole.shape, BF16),
            pltpu.SemaphoreType.DMA((7,)),
            pltpu.SemaphoreType.DMA((BLOCKS,)),
        ],
        compiler_params=pltpu.CompilerParams(vmem_limit_bytes=60 * 2**20),
    )(lead_whole, panel_block, far, charge_whole, trailing_slab, charge_rest))


def solution(mesh):
    placed = (P("row", None), P("row", None), P("row", "col"), P("row", "col"), P("row", "col"))
    return jax.shard_map(shards, mesh=mesh, in_specs=placed, out_specs=placed, check_vma=False)
```

time: 102 us -> 82.9 us (0.81)
  the two profiles are of different devices: /device:TPU:139 before, /device:TPU:1 now
where the time goes in v3:
time: 82.9 us; the launch traced here: 81.8 us
  Pallas kernels  81 us (98%)
    pallas_call x1, Pallas kernels, gathered(): pl.pallas_call(gather, out_shape=[tall(lead_block), jax.ShapeDtypeStruct(...  45.7 us
    pallas_call x1, Pallas kernels, shards(): pl.pallas_call(kernel, out_shape=[like(lead_block), like(panel_block), li...  35.2 us

profile of v3, /device:TPU:1, one launch (start us, length us, event | category | flops | bytes accessed | tf_op | source)
XLA Modules:
  0.0 81.8 jit_solution(3234095421718297164)
XLA Ops:
  0.6 45.7 %shard_map.92 = (f32[1024,1024]{1,0:T(8,128)}, f32[512,1024]{1,0:T(8,128)}, f32[1024,128]{1,0:T(8,128)}) custom-call(f32[32,1024]{1,0:T(8,128)} %lead.1, f32[512,1024]{1,0:T(8,128)} %panel.3, f32[32,128]{1,0:T(8,128)} %charge.1), custom_call_target="tpu_custom_call" | custom-call | tf_op jit(solution)/shard_map/pallas_call | solution.py:447
  46.4 35.2 %shard_map.93 = (f32[32,1024]{1,0:T(8,128)}, f32[512,1024]{1,0:T(8,128)}, f32[512,512]{1,0:T(8,128)}, f32[32,128]{1,0:T(8,128)}, f32[512,128]{1,0:T(8,128)}) custom-call(f32[1024,1024]{1,0:T(8,128)} %get-tuple-element.8.lead, f32[512,1024]{1,0:T(8,128)} %panel.3, f32[512,1024]{1,0:T(8,128)} %get-tuple-element.9.far, f32[1024,128]{1,0:T(8,128)} %get-tuple-element.10.charge, ...), custom_call_target="tpu_custom_call" | custom-call | tf_op jit(solution)/shard_map/pallas_call | solution.py:464
